TPU v7x, 32 devices: a whole 2x2x4 slice. The times are simulated.
32 devices in a mesh: runs: 2 (over x), tm: 16 (over z, y, core), pix: 1.
Axes of the slice: x: 2, y: 2, z: 4, core: 2. Of those that a mesh axis runs over, the one named last changes fastest.
Arguments:
- intensity: float32 [2048, 4096], P('tm', ('runs', 'pix')), parts along dimension 1, may hold values from 0.01 to 60
- cycle_label: int32 [4096], P(('runs', 'pix')), parts along dimension 0, may hold values from 0 to 127, as said below
- valid_mask: int32 [4096], P(('runs', 'pix')), parts along dimension 0, may hold values from 0 to 1, as said below
Outputs:
- correlation: float32 [128, 4096], P('tm', ('runs', 'pix')), parts along dimension 1
There are 2 independent parts, one for each index of `runs`. A program takes and returns all parts, laid end to end along the dimension named above; each array names one. Nothing has to cross between parts.
Inputs may be any that keep to these rules, and one draw needn't show every extreme that they name: `cycle_label`: every cycle 0 to 127 is the label of exactly 16 pixels. `valid_mask`: every cycle holds at least one pixel marked 1.
All inputs are finite; a program needn't handle non-finite values.
Results may differ from a plain program's by a relative error of at most 0.0001.
Values sent between devices are 32-bit elements; how exact they have to be, the bound alone decides.
A program may use at most 64 MiB of HBM per device.

v0:
```python
import jax
import jax.numpy as jnp
from jax import lax
from jax.sharding import PartitionSpec as P

Q = 128
LEVELS = 8
LAGS = 16


def coarsen(series):
    paired = series.reshape(series.shape[0] // 2, 2, series.shape[1])
    return (paired[:, 0] + paired[:, 1]) * 0.5


def level_rows(series, extension, total_frames):
    frames_here = series.shape[0]
    row_list = []
    for offset in range(extension.shape[0] + 1):
        inside = min(offset, frames_here)
        total = jnp.sum(series[: frames_here - inside] * series[inside:], axis=0)
        if offset > 0:
            tail_rows = series[frames_here - inside :]
            total = total + jnp.sum(tail_rows * extension[offset - inside : offset], axis=0)
        row_list.append(total / (total_frames - offset))
    return row_list


def pixel_rows(gathered):
    series = gathered[:, 0, :]
    row_list = []
    for height in range(LEVELS):
        if height > 0:
            series = coarsen(series)
        extension = jnp.zeros((LAGS - 1, series.shape[1]), jnp.float32)
        row_list = row_list + level_rows(series, extension, series.shape[0])
    return jnp.stack(row_list)


def body(intensity, cycle_label, valid_mask):
    valid_flag = valid_mask.astype(jnp.float32)
    member = (cycle_label[:, None] == jnp.arange(Q, dtype=jnp.int32)[None, :]).astype(jnp.float32)
    weighted = member * valid_flag[:, None]
    partial_sum = jnp.dot(intensity, weighted, precision=lax.Precision.HIGHEST)
    partial_count = jnp.sum(weighted, axis=0)
    cycle_sum, cycle_count = lax.psum((partial_sum, partial_count), "pix")
    cycle_mean = cycle_sum / cycle_count[None, :]
    per_pixel = lax.dot_general(
        cycle_mean, member, (((1,), (1,)), ((), ())), precision=lax.Precision.HIGHEST
    )
    normed = valid_flag[None, :] * intensity / per_pixel
    devices_tm = lax.axis_size("tm")
    tile_width = normed.shape[1] // devices_tm
    pieces = normed.reshape(normed.shape[0], devices_tm, tile_width)
    rows_local = pixel_rows(lax.all_to_all(pieces, "tm", split_axis=1, concat_axis=0, tiled=True))
    return lax.all_to_all(rows_local, "tm", split_axis=0, concat_axis=1, tiled=True)


def solution(mesh):
    placed = (P("tm", ("runs", "pix")), P(("runs", "pix")), P(("runs", "pix")))
    return jax.shard_map(
        body, mesh=mesh, in_specs=placed, out_specs=P("tm", ("runs", "pix")), check_vma=False
    )
```

profile of v0, /device:TPU:0, one launch (start us, length us, event | category | flops | bytes accessed | tf_op | source)
XLA Modules:
  0.0 95.0 jit_solution(12186441031817750926)
XLA Ops:
  0.0 0.8 convert_element_type.4
  0.8 0.7 select_reduce_fusion
  1.5 3.6 %fusion.3 = f32[128,128]{1,0:T(8,128)S(1)} fusion(f32[128,2048]{1,0:T(8,128)} %param.3, f32[2048]{0:T(1024)S(1)} %convert_element_type.4, s32[2048]{0:T(1024)S(1)} %copy-done, f32[128]{0:T(128)S(1)} %select_reduce_fusion), kind=kOutput, calls=%fused_computation.5 | convolution fusion | flops 403193856 | bytes 1131008 | tf_op jit(solution)/shard_map/dot_general | solution.py:44
  5.1 1.2 %fusion.2 = f32[16,16,8,128]{3,2,1,0:T(8,128)S(1)} fusion(f32[128,128]{1,0:T(8,128)S(1)} %fusion.3, f32[128,2048]{1,0:T(8,128)S(1)} %copy-done.1, s32[2048]{0:T(1024)S(1)} %copy-done, f32[2048]{0:T(1024)S(1)} %convert_element_type.4), kind=kOutput, calls=%fused_computation.4 | convolution fusion | flops 403439616 | bytes 2179072 | tf_op jit(solution)/shard_map/dot_general | solution.py:48
  6.5 31.9 %all_to_all.34 = f32[128,16,128]{2,0,1:T(8,128)S(1)} all-to-all(f32[128,16,128]{2,0,1:T(8,128)S(1)} %bitcast.378), channel_id=1, replica_groups=mesh['runs'=2,'tm'=16,'pix'=1] {'tm'}, dimensions={1} | all-to-all | bytes 2097152 | tf_op jit(solution)/shard_map/all_to_all | solution.py:55
  43.0 1.2 %multiply_reduce_fusion = (f32[128]{0:T(128)S(1)}, f32[1024,1,128]{2,1,0:T(1,128)S(1)}) fusion(f32[1024,2,128]{2,1,0:T(2,128)S(1)} %bitcast.370), kind=kLoop, calls=%fused_computation.42 | loop fusion | flops 524160 | bytes 1573376 | tf_op jit(solution)/shard_map/reduce_sum | solution.py:21
  44.2 1.1 %fusion.36 = f32[128]{0:T(128)S(1)} fusion(f32[1024,1,128]{2,1,0:T(1,128)S(1)} %get-tuple-element.46), kind=kLoop, calls=%fused_computation.66 | loop fusion | flops 259456 | bytes 1038848 | tf_op jit(solution)/shard_map/reduce_sum | solution.py:21
  45.3 1.1 %fusion.38 = f32[128]{0:T(128)S(1)} fusion(f32[1024,1,128]{2,1,0:T(1,128)S(1)} %get-tuple-element.46), kind=kLoop, calls=%fused_computation.70 | loop fusion | flops 258944 | bytes 1036800 | tf_op jit(solution)/shard_map/reduce_sum | solution.py:21
  46.4 1.1 %fusion.35 = f32[128]{0:T(128)S(1)} fusion(f32[1024,1,128]{2,1,0:T(1,128)S(1)} %get-tuple-element.46), kind=kLoop, calls=%fused_computation.64 | loop fusion | flops 259712 | bytes 1039872 | tf_op jit(solution)/shard_map/reduce_sum | solution.py:21
  47.5 1.1 %fusion.39 = f32[128]{0:T(128)S(1)} fusion(f32[1024,1,128]{2,1,0:T(1,128)S(1)} %get-tuple-element.46), kind=kLoop, calls=%fused_computation.72 | loop fusion | flops 258688 | bytes 1035776 | tf_op jit(solution)/shard_map/reduce_sum | solution.py:21
  48.6 1.1 %fusion.34 = f32[128]{0:T(128)S(1)} fusion(f32[1024,1,128]{2,1,0:T(1,128)S(1)} %get-tuple-element.46), kind=kLoop, calls=%fused_computation.62 | loop fusion | flops 259968 | bytes 1040896 | tf_op jit(solution)/shard_map/reduce_sum | solution.py:21
  49.8 1.1 %fusion.33 = f32[128]{0:T(128)S(1)} fusion(f32[1024,1,128]{2,1,0:T(1,128)S(1)} %get-tuple-element.46), kind=kLoop, calls=%fused_computation.60 | loop fusion | flops 260224 | bytes 1041920 | tf_op jit(solution)/shard_map/reduce_sum | solution.py:21
  50.9 1.1 %fusion.32 = f32[128]{0:T(128)S(1)} fusion(f32[1024,1,128]{2,1,0:T(1,128)S(1)} %get-tuple-element.46), kind=kLoop, calls=%fused_computation.58 | loop fusion | flops 260480 | bytes 1042944 | tf_op jit(solution)/shard_map/reduce_sum | solution.py:21
  52.0 1.1 %fusion.40 = f32[128]{0:T(128)S(1)} fusion(f32[1024,1,128]{2,1,0:T(1,128)S(1)} %get-tuple-element.46), kind=kLoop, calls=%fused_computation.74 | loop fusion | flops 258432 | bytes 1034752 | tf_op jit(solution)/shard_map/reduce_sum | solution.py:21
  53.1 1.1 %fusion.31 = f32[128]{0:T(128)S(1)} fusion(f32[1024,1,128]{2,1,0:T(1,128)S(1)} %get-tuple-element.46), kind=kLoop, calls=%fused_computation.56 | loop fusion | flops 260736 | bytes 1043968 | tf_op jit(solution)/shard_map/reduce_sum | solution.py:21
  54.2 1.1 %fusion.30 = f32[128]{0:T(128)S(1)} fusion(f32[1024,1,128]{2,1,0:T(1,128)S(1)} %get-tuple-element.46), kind=kLoop, calls=%fused_computation.54 | loop fusion | flops 260992 | bytes 1044992 | tf_op jit(solution)/shard_map/reduce_sum | solution.py:21
  55.3 1.3 %fusion.37 = f32[128]{0:T(128)S(1)} fusion(f32[1024,1,128]{2,1,0:T(1,128)S(1)} %get-tuple-element.46), kind=kLoop, calls=%fused_computation.68 | loop fusion | flops 259200 | bytes 1037824 | tf_op jit(solution)/shard_map/reduce_sum | solution.py:21
  56.6 1.1 %fusion.29 = f32[128]{0:T(128)S(1)} fusion(f32[1024,1,128]{2,1,0:T(1,128)S(1)} %get-tuple-element.46), kind=kLoop, calls=%fused_computation.52 | loop fusion | flops 261248 | bytes 1046016 | tf_op jit(solution)/shard_map/reduce_sum | solution.py:21
  57.7 1.1 %fusion.41 = f32[128]{0:T(128)S(1)} fusion(f32[1024,1,128]{2,1,0:T(1,128)S(1)} %get-tuple-element.46), kind=kLoop, calls=%fused_computation.76 | loop fusion | flops 258176 | bytes 1033728 | tf_op jit(solution)/shard_map/reduce_sum | solution.py:21
  58.8 1.1 %fusion.28 = f32[128]{0:T(128)S(1)} fusion(f32[1024,1,128]{2,1,0:T(1,128)S(1)} %get-tuple-element.46), kind=kLoop, calls=%fused_computation.50 | loop fusion | flops 261504 | bytes 1047040 | tf_op jit(solution)/shard_map/reduce_sum | solution.py:21
  60.0 1.1 %fusion.27 = f32[128]{0:T(128)S(1)} fusion(f32[1024,1,128]{2,1,0:T(1,128)S(1)} %get-tuple-element.46), kind=kLoop, calls=%fused_computation.48 | loop fusion | flops 261760 | bytes 1048064 | tf_op jit(solution)/shard_map/reduce_sum | solution.py:21
  61.1 0.6 multiply_reduce_fusion.1
  63.9 0.5 fusion.50
  64.5 0.5 fusion.49
  65.1 0.5 fusion.48
  66.2 0.6 fusion.47
  66.9 0.6 fusion.46
  68.0 0.6 fusion.45
  69.1 0.6 fusion.44
  69.7 0.6 fusion.43
  82.6 11.7 %all_to_all.35 = f32[16,8,128]{2,1,0:T(8,128)S(1)} all-to-all(f32[16,8,128]{2,1,0:T(8,128)S(1)} %bitcast.379), channel_id=1, replica_groups=mesh['runs'=2,'tm'=16,'pix'=1] {'tm'}, dimensions={0} | all-to-all | bytes 131072 | tf_op jit(solution)/shard_map/all_to_all | solution.py:56
  94.4 0.6 copy.12
  (270 shorter events, 21.1 us)
Async XLA Ops:
  0.0 0.8 copy-start
  0.0 5.1 %copy-start.1 = (f32[128,2048]{1,0:T(8,128)S(1)}, f32[128,2048]{1,0:T(8,128)}, u32[]{:S(2)}) copy-start(f32[128,2048]{1,0:T(8,128)} %param.3) | copy-start | bytes 3145732
where the time goes:
time: 95.3 us; the launch traced here: 95 us
  other arithmetic  44.8 us (47%)
  blocking collectives  43.6 us (46%)
  matrix products  4.86 us (5%)
  local copies, waits for them, and re-layouts  1.1 us (1%)
    reduce_sum x119, other arithmetic, level_rows(): total = jnp.sum(series[:frames_here - inside] * series[inside:], axis=0)  40.1 us
    all_to_all x1, blocking collectives, body(): lax.all_to_all(pieces, 'tm', split_axis=1, concat_axis=0, tiled=True)  31.9 us
    all_to_all x1, blocking collectives, body(): lax.all_to_all(rows_local, 'tm', split_axis=0, concat_axis=1, tiled=True)  11.7 us
    dot_general x1, matrix products, body(): partial_sum = jnp.dot(intensity, weighted, precision=lax.Precision.HIGHEST)  3.63 us
    reduce_sum x106, other arithmetic, level_rows(): jnp.sum(tail_rows * extension[offset - inside:offset], axis=0)  2.74 us

commit v1 on v0

--- a/solution.py
+++ b/solution.py
@@ -6,6 +6,34 @@
 Q = 128
 LEVELS = 8
 LAGS = 16
+
+
+def match_lanes_here(message, dim_no, shard_in):
+    y1, outcome_arr = (message.shape[:dim_no], message.shape[dim_no + 1 :])
+    now = message.reshape(*y1, shard_in, -1, *outcome_arr)
+    return jnp.moveaxis(now, dim_no, 0)
+
+
+def sample_obtain(s0, dim_k):
+    s0 = jnp.moveaxis(s0, 0, dim_k)
+    local_next = s0.shape
+    return s0.reshape(
+        *local_next[:dim_k], local_next[dim_k] * local_next[dim_k + 1], *local_next[dim_k + 2 :]
+    )
+
+
+def pair_flows(vals, device_axis, arr_in, block_in):
+    x_now = lax.psum(1, device_axis)
+    odd, out_arr = (x_now, lax.axis_index(device_axis))
+    arr_now = match_lanes_here(vals, arr_in, odd)
+    rack = [arr_now[out_arr]]
+    for nth in tuple(range(1, odd)):
+        part_now = arr_now[(out_arr + nth) % odd]
+        arr_out = lax.ppermute(part_now, device_axis, [(p, (p + nth) % odd) for p in range(odd)])
+        rack.append(arr_out)
+    b_next = jnp.stack(rack)
+    arr_now = b_next[(out_arr - jnp.arange(odd)) % odd]
+    return sample_obtain(arr_now, block_in)
 
 
 def coarsen(series):
@@ -52,7 +80,7 @@
     devices_tm = lax.axis_size("tm")
     tile_width = normed.shape[1] // devices_tm
     pieces = normed.reshape(normed.shape[0], devices_tm, tile_width)
-    rows_local = pixel_rows(lax.all_to_all(pieces, "tm", split_axis=1, concat_axis=0, tiled=True))
+    rows_local = pixel_rows(pair_flows(pieces, "tm", 1, 0))
     return lax.all_to_all(rows_local, "tm", split_axis=0, concat_axis=1, tiled=True)
 
 

time: 95.3 us -> 98.4 us (1.033)
  blocking collectives: 43.6 us -> 12.7 us
  starting transfers between devices: 0 us -> 21.9 us
  waiting for transfers between devices: 0 us -> 9.47 us
  local copies, waits for them, and re-layouts: 1.1 us -> 4.27 us
    all_to_all x1 -> x0, blocking collectives: 31.9 us -> none  [body(): lax.all_to_all(pieces, 'tm', split_axis=1, concat_axis=0, tiled=True)]
    ppermute x0 -> x15, starting transfers between devices: none -> 21.9 us  [pair_flows(): lax.ppermute(part_now, device_axis, [(p, (p + nth) % odd) for p in range(...]
    ppermute x0 -> x15, waiting for transfers between devices: none -> 9.47 us  [pair_flows(): lax.ppermute(part_now, device_axis, [(p, (p + nth) % odd) for p in range(...]
    unnamed x5 -> x23, local copies, waits for them, and re-layouts: 0.64 us -> 2.3 us
    another operation x0 -> x2, local copies, waits for them, and re-layouts: none -> 0.99 us
  transfers between devices with their start and end apart: 0 -> 15, of which waited for: 0 -> 5; matrix products, arithmetic and copies ran while one was open for 0% -> 0% of each run, Pallas kernels for 0% -> 0%
where the time goes in v1:
time: 98.4 us; the launch traced here: 98.1 us
  other arithmetic  44.1 us (45%)
  starting transfers between devices  21.9 us (22%)
  blocking collectives  12.7 us (13%)
  waiting for transfers between devices  9.47 us (10%)
  matrix products  4.88 us (5%)
  local copies, waits for them, and re-layouts  4.27 us (4%)
    reduce_sum x119, other arithmetic, level_rows(): total = jnp.sum(series[:frames_here - inside] * series[inside:], axis=0)  40.1 us
    ppermute x15, starting transfers between devices, pair_flows(): lax.ppermute(part_now, device_axis, [(p, (p + nth) % odd) for p in range(...  21.9 us
    all_to_all x1, blocking collectives, body(): lax.all_to_all(rows_local, 'tm', split_axis=0, concat_axis=1, tiled=True)  12.7 us
    ppermute x15, waiting for transfers between devices, pair_flows(): lax.ppermute(part_now, device_axis, [(p, (p + nth) % odd) for p in range(...  9.47 us
    dot_general x1, matrix products, body(): partial_sum = jnp.dot(intensity, weighted, precision=lax.Precision.HIGHEST)  3.63 us
    reduce_sum x106, other arithmetic, level_rows(): jnp.sum(tail_rows * extension[offset - inside:offset], axis=0)  2.74 us
    unnamed x23, local copies, waits for them, and re-layouts  2.3 us
  transfers between devices with their start and end apart: 15, of which 5 were waited for; matrix products, arithmetic and copies ran while one was open for 0% of the time, Pallas kernels for 0%

profile of v1, /device:TPU:0, one launch (start us, length us, event | category | flops | bytes accessed | tf_op | source)
XLA Modules:
  0.0 98.1 jit_solution(9811610050498867715)
XLA Ops:
  1.4 0.7 select_reduce_fusion
  2.1 3.6 %fusion.3 = f32[128,128]{1,0:T(8,128)S(1)} fusion(f32[128,2048]{1,0:T(8,128)} %param.3, f32[2048]{0:T(1024)S(1)} %convert_element_type.4, s32[2048]{0:T(1024)S(1)} %copy-done.1, f32[128]{0:T(128)S(1)} %select_reduce_fusion), kind=kOutput, calls=%fused_computation.6 | convolution fusion | flops 403193856 | bytes 1131008 | tf_op jit(solution)/shard_map/dot_general | solution.py:72
  5.7 1.3 %fusion.2 = f32[16,8,16,128]{3,1,2,0:T(8,128)S(1)} fusion(f32[128,128]{1,0:T(8,128)S(1)} %fusion.3, f32[128,2048]{1,0:T(8,128)S(1)} %copy-done.2, s32[2048]{0:T(1024)S(1)} %copy-done.1, f32[2048]{0:T(1024)S(1)} %convert_element_type.4), kind=kOutput, calls=%fused_computation.5 | convolution fusion | flops 403439616 | bytes 2179072 | tf_op jit(solution)/shard_map/dot_general | solution.py:76
  7.3 1.0 %constant_dynamic-slice_fusion = (f32[128,1,1,128]{3,1,0,2:T(1,128)S(1)}, f32[128,1,1,128]{3,1,0,2:T(1,128)S(1)}, f32[128,1,1,128]{3,1,0,2:T(1,128)S(1)}, f32[12...) fusion(f32[128,16,1,128]{3,1,0,2:T(8,128)S(1)} %bitcast.419, ...), kind=kLoop, calls=%fused_computation.396 | loop fusion | bytes 2097216 | tf_op jit(solution)/shard_map/dynamic-slice.15
  8.8 2.6 %collective-permute-start.1 = (f32[128,1,128]{2,0,1:T(8,128)S(1)}, f32[128,1,128]{2,0,1:T(8,128)S(1)}, u32[]{:S(2)}, u32[]{:S(2)}) collective-permute-start(f32[128,1,128]{2,0,1:T(8,128)S(1)} %bitcast.437), channel_id=1, source_target_pairs={{0,2},{1,3},{2,4},{3,5},{4,6},{5,7},{6,8},{7,9},{8,10},{9,11},{10,... | collective-permute-start | bytes 196616 | tf_op jit(solution)/shard_map/ppermute | solution.py:32
  11.4 2.4 %collective-permute-start.2 = (f32[128,1,128]{2,0,1:T(8,128)S(1)}, f32[128,1,128]{2,0,1:T(8,128)S(1)}, u32[]{:S(2)}, u32[]{:S(2)}) collective-permute-start(f32[128,1,128]{2,0,1:T(8,128)S(1)} %bitcast.436), channel_id=1, source_target_pairs={{0,3},{1,4},{2,5},{3,6},{4,7},{5,8},{6,9},{7,10},{8,11},{9,12},{10... | collective-permute-start | bytes 196616 | tf_op jit(solution)/shard_map/ppermute | solution.py:32
  13.8 1.6 %collective-permute-start.3 = (f32[128,1,128]{2,0,1:T(8,128)S(1)}, f32[128,1,128]{2,0,1:T(8,128)S(1)}, u32[]{:S(2)}, u32[]{:S(2)}) collective-permute-start(f32[128,1,128]{2,0,1:T(8,128)S(1)} %bitcast.435), channel_id=1, source_target_pairs={{0,4},{1,5},{2,6},{3,7},{4,8},{5,9},{6,10},{7,11},{8,12},{9,13},{1... | collective-permute-start | bytes 196616 | tf_op jit(solution)/shard_map/ppermute | solution.py:32
  15.7 1.1 %collective-permute-start.5 = (f32[128,1,128]{2,0,1:T(8,128)S(1)}, f32[128,1,128]{2,0,1:T(8,128)S(1)}, u32[]{:S(2)}, u32[]{:S(2)}) collective-permute-start(f32[128,1,128]{2,0,1:T(8,128)S(1)} %bitcast.433), channel_id=1, source_target_pairs={{0,6},{1,7},{2,8},{3,9},{4,10},{5,11},{6,12},{7,13},{8,14},{9,15},... | collective-permute-start | bytes 196616 | tf_op jit(solution)/shard_map/ppermute | solution.py:32
  16.8 4.4 %collective-permute-start.6 = (f32[128,1,128]{2,0,1:T(8,128)S(1)}, f32[128,1,128]{2,0,1:T(8,128)S(1)}, u32[]{:S(2)}, u32[]{:S(2)}) collective-permute-start(f32[128,1,128]{2,0,1:T(8,128)S(1)} %bitcast.432), channel_id=1, source_target_pairs={{0,7},{1,8},{2,9},{3,10},{4,11},{5,12},{6,13},{7,14},{8,15},{9,0},... | collective-permute-start | bytes 196616 | tf_op jit(solution)/shard_map/ppermute | solution.py:32
  22.0 6.5 %collective-permute-done.4 = f32[128,1,128]{2,0,1:T(8,128)S(1)} collective-permute-done((f32[128,1,128]{2,0,1:T(8,128)S(1)}, f32[128,1,128]{2,0,1:T(8,128)S(1)}, u32[]{:S(2)}, u32[]{:S(2)}) %collective-permute-start.4) | collective-permute-done | bytes 65568 | tf_op jit(solution)/shard_map/ppermute | solution.py:32
  29.2 1.9 %collective-permute-start.11 = (f32[128,1,128]{2,0,1:T(8,128)S(1)}, f32[128,1,128]{2,0,1:T(8,128)S(1)}, u32[]{:S(2)}, u32[]{:S(2)}) collective-permute-start(f32[128,1,128]{2,0,1:T(8,128)S(1)} %bitcast.427), channel_id=1, source_target_pairs={{0,12},{1,13},{2,14},{3,15},{4,0},{5,1},{6,2},{7,3},{8,4},{9,5},{1... | collective-permute-start | bytes 196616 | tf_op jit(solution)/shard_map/ppermute | solution.py:32
  31.0 2.2 %collective-permute-start.12 = (f32[128,1,128]{2,0,1:T(8,128)S(1)}, f32[128,1,128]{2,0,1:T(8,128)S(1)}, u32[]{:S(2)}, u32[]{:S(2)}) collective-permute-start(f32[128,1,128]{2,0,1:T(8,128)S(1)} %bitcast.426), channel_id=1, source_target_pairs={{0,13},{1,14},{2,15},{3,0},{4,1},{5,2},{6,3},{7,4},{8,5},{9,6},{10... | collective-permute-start | bytes 196616 | tf_op jit(solution)/shard_map/ppermute | solution.py:32
  33.3 3.4 %collective-permute-start.13 = (f32[128,1,128]{2,0,1:T(8,128)S(1)}, f32[128,1,128]{2,0,1:T(8,128)S(1)}, u32[]{:S(2)}, u32[]{:S(2)}) collective-permute-start(f32[128,1,128]{2,0,1:T(8,128)S(1)} %bitcast.425), channel_id=1, source_target_pairs={{0,14},{1,15},{2,0},{3,1},{4,2},{5,3},{6,4},{7,5},{8,6},{9,7},{10,... | collective-permute-start | bytes 196616 | tf_op jit(solution)/shard_map/ppermute | solution.py:32
  37.3 2.1 %collective-permute-done.13 = f32[128,1,128]{2,0,1:T(8,128)S(1)} collective-permute-done((f32[128,1,128]{2,0,1:T(8,128)S(1)}, f32[128,1,128]{2,0,1:T(8,128)S(1)}, u32[]{:S(2)}, u32[]{:S(2)}) %collective-permute-start.13) | collective-permute-done | bytes 65568 | tf_op jit(solution)/shard_map/ppermute | solution.py:32
  40.5 1.2 %multiply_reduce_fusion.1 = (f32[128]{0:T(128)S(1)}, f32[1024,1,128]{2,1,0:T(1,128)S(1)}) fusion(f32[1024,2,128]{2,1,0:T(2,128)S(1)} %bitcast.382), kind=kLoop, calls=%fused_computation.41 | loop fusion | flops 524160 | bytes 1573376 | tf_op jit(solution)/shard_map/reduce_sum | solution.py:49
  58.1 0.8 fusion.48
  61.2 1.1 %fusion.40 = f32[128]{0:T(128)S(1)} fusion(f32[1024,1,128]{2,1,0:T(1,128)S(1)} %get-tuple-element.46), kind=kLoop, calls=%fused_computation.75 | loop fusion | flops 258176 | bytes 1033728 | tf_op jit(solution)/shard_map/reduce_sum | solution.py:49
  62.3 1.1 %fusion.38 = f32[128]{0:T(128)S(1)} fusion(f32[1024,1,128]{2,1,0:T(1,128)S(1)} %get-tuple-element.46), kind=kLoop, calls=%fused_computation.71 | loop fusion | flops 258688 | bytes 1035776 | tf_op jit(solution)/shard_map/reduce_sum | solution.py:49
  63.4 1.1 %fusion.39 = f32[128]{0:T(128)S(1)} fusion(f32[1024,1,128]{2,1,0:T(1,128)S(1)} %get-tuple-element.46), kind=kLoop, calls=%fused_computation.73 | loop fusion | flops 258432 | bytes 1034752 | tf_op jit(solution)/shard_map/reduce_sum | solution.py:49
  64.5 1.1 %fusion.36 = f32[128]{0:T(128)S(1)} fusion(f32[1024,1,128]{2,1,0:T(1,128)S(1)} %get-tuple-element.46), kind=kLoop, calls=%fused_computation.67 | loop fusion | flops 259200 | bytes 1037824 | tf_op jit(solution)/shard_map/reduce_sum | solution.py:49
  65.6 1.1 %fusion.37 = f32[128]{0:T(128)S(1)} fusion(f32[1024,1,128]{2,1,0:T(1,128)S(1)} %get-tuple-element.46), kind=kLoop, calls=%fused_computation.69 | loop fusion | flops 258944 | bytes 1036800 | tf_op jit(solution)/shard_map/reduce_sum | solution.py:49
  66.8 1.1 %fusion.34 = f32[128]{0:T(128)S(1)} fusion(f32[1024,1,128]{2,1,0:T(1,128)S(1)} %get-tuple-element.46), kind=kLoop, calls=%fused_computation.63 | loop fusion | flops 259712 | bytes 1039872 | tf_op jit(solution)/shard_map/reduce_sum | solution.py:49
  67.8 1.1 %fusion.35 = f32[128]{0:T(128)S(1)} fusion(f32[1024,1,128]{2,1,0:T(1,128)S(1)} %get-tuple-element.46), kind=kLoop, calls=%fused_computation.65 | loop fusion | flops 259456 | bytes 1038848 | tf_op jit(solution)/shard_map/reduce_sum | solution.py:49
  69.0 1.1 %fusion.32 = f32[128]{0:T(128)S(1)} fusion(f32[1024,1,128]{2,1,0:T(1,128)S(1)} %get-tuple-element.46), kind=kLoop, calls=%fused_computation.59 | loop fusion | flops 260224 | bytes 1041920 | tf_op jit(solution)/shard_map/reduce_sum | solution.py:49
  70.1 1.1 %fusion.33 = f32[128]{0:T(128)S(1)} fusion(f32[1024,1,128]{2,1,0:T(1,128)S(1)} %get-tuple-element.46), kind=kLoop, calls=%fused_computation.61 | loop fusion | flops 259968 | bytes 1040896 | tf_op jit(solution)/shard_map/reduce_sum | solution.py:49
  71.2 1.1 %fusion.30 = f32[128]{0:T(128)S(1)} fusion(f32[1024,1,128]{2,1,0:T(1,128)S(1)} %get-tuple-element.46), kind=kLoop, calls=%fused_computation.55 | loop fusion | flops 260736 | bytes 1043968 | tf_op jit(solution)/shard_map/reduce_sum | solution.py:49
  72.3 1.1 %fusion.31 = f32[128]{0:T(128)S(1)} fusion(f32[1024,1,128]{2,1,0:T(1,128)S(1)} %get-tuple-element.46), kind=kLoop, calls=%fused_computation.57 | loop fusion | flops 260480 | bytes 1042944 | tf_op jit(solution)/shard_map/reduce_sum | solution.py:49
  73.4 1.1 %fusion.28 = f32[128]{0:T(128)S(1)} fusion(f32[1024,1,128]{2,1,0:T(1,128)S(1)} %get-tuple-element.46), kind=kLoop, calls=%fused_computation.51 | loop fusion | flops 261248 | bytes 1046016 | tf_op jit(solution)/shard_map/reduce_sum | solution.py:49
  74.5 1.1 %fusion.29 = f32[128]{0:T(128)S(1)} fusion(f32[1024,1,128]{2,1,0:T(1,128)S(1)} %get-tuple-element.46), kind=kLoop, calls=%fused_computation.53 | loop fusion | flops 260992 | bytes 1044992 | tf_op jit(solution)/shard_map/reduce_sum | solution.py:49
  76.2 1.1 %fusion.26 = f32[128]{0:T(128)S(1)} fusion(f32[1024,1,128]{2,1,0:T(1,128)S(1)} %get-tuple-element.46), kind=kLoop, calls=%fused_computation.47 | loop fusion | flops 261760 | bytes 1048064 | tf_op jit(solution)/shard_map/reduce_sum | solution.py:49
  77.3 1.1 %fusion.27 = f32[128]{0:T(128)S(1)} fusion(f32[1024,1,128]{2,1,0:T(1,128)S(1)} %get-tuple-element.46), kind=kLoop, calls=%fused_computation.49 | loop fusion | flops 261504 | bytes 1047040 | tf_op jit(solution)/shard_map/reduce_sum | solution.py:49
  84.8 12.7 %all_to_all.19 = f32[16,8,128]{2,1,0:T(8,128)S(1)} all-to-all(f32[16,8,128]{2,1,0:T(8,128)S(1)} %bitcast.422), channel_id=1, replica_groups=mesh['runs'=2,'tm'=16,'pix'=1] {'tm'}, dimensions={0} | all-to-all | bytes 131072 | tf_op jit(solution)/shard_map/all_to_all | solution.py:84
  (321 shorter events, 31.7 us)
Async XLA Ops:
  0.0 0.7 copy-start
  0.7 0.7 copy-start.1
  0.7 5.0 %copy-start.2 = (f32[128,2048]{1,0:T(8,128)S(1)}, f32[128,2048]{1,0:T(8,128)}, u32[]{:S(2)}) copy-start(f32[128,2048]{1,0:T(8,128)} %param.3) | copy-start | bytes 3145732
  8.3 7.5 %collective-permute-start = (f32[128,1,128]{2,0,1:T(8,128)S(1)}, f32[128,1,128]{2,0,1:T(8,128)S(1)}, u32[]{:S(2)}, u32[]{:S(2)}) collective-permute-start(f32[128,1,128]{2,0,1:T(8,128)S(1)} %bitcast.438), channel_id=1, source_target_pairs={{0,1},{1,2},{2,3},{3,4},{4,5},{5,6},{6,7},{7,8},{8,9},{9,10},{10,1... | collective-permute-start | bytes 196616 | tf_op jit(solution)/shard_map/ppermute | solution.py:32
  8.8 8.0 %collective-permute-start.1 = (f32[128,1,128]{2,0,1:T(8,128)S(1)}, f32[128,1,128]{2,0,1:T(8,128)S(1)}, u32[]{:S(2)}, u32[]{:S(2)}) collective-permute-start(f32[128,1,128]{2,0,1:T(8,128)S(1)} %bitcast.437), channel_id=1, source_target_pairs={{0,2},{1,3},{2,4},{3,5},{4,6},{5,7},{6,8},{7,9},{8,10},{9,11},{10,... | collective-permute-start | bytes 196616 | tf_op jit(solution)/shard_map/ppermute | solution.py:32
  11.4 9.9 %collective-permute-start.2 = (f32[128,1,128]{2,0,1:T(8,128)S(1)}, f32[128,1,128]{2,0,1:T(8,128)S(1)}, u32[]{:S(2)}, u32[]{:S(2)}) collective-permute-start(f32[128,1,128]{2,0,1:T(8,128)S(1)} %bitcast.436), channel_id=1, source_target_pairs={{0,3},{1,4},{2,5},{3,6},{4,7},{5,8},{6,9},{7,10},{8,11},{9,12},{10... | collective-permute-start | bytes 196616 | tf_op jit(solution)/shard_map/ppermute | solution.py:32
  13.8 7.9 %collective-permute-start.3 = (f32[128,1,128]{2,0,1:T(8,128)S(1)}, f32[128,1,128]{2,0,1:T(8,128)S(1)}, u32[]{:S(2)}, u32[]{:S(2)}) collective-permute-start(f32[128,1,128]{2,0,1:T(8,128)S(1)} %bitcast.435), channel_id=1, source_target_pairs={{0,4},{1,5},{2,6},{3,7},{4,8},{5,9},{6,10},{7,11},{8,12},{9,13},{1... | collective-permute-start | bytes 196616 | tf_op jit(solution)/shard_map/ppermute | solution.py:32
  15.4 13.2 %collective-permute-start.4 = (f32[128,1,128]{2,0,1:T(8,128)S(1)}, f32[128,1,128]{2,0,1:T(8,128)S(1)}, u32[]{:S(2)}, u32[]{:S(2)}) collective-permute-start(f32[128,1,128]{2,0,1:T(8,128)S(1)} %bitcast.434), channel_id=1, source_target_pairs={{0,5},{1,6},{2,7},{3,8},{4,9},{5,10},{6,11},{7,12},{8,13},{9,14},{... | collective-permute-start | bytes 196616 | tf_op jit(solution)/shard_map/ppermute | solution.py:32
  15.7 13.0 %collective-permute-start.5 = (f32[128,1,128]{2,0,1:T(8,128)S(1)}, f32[128,1,128]{2,0,1:T(8,128)S(1)}, u32[]{:S(2)}, u32[]{:S(2)}) collective-permute-start(f32[128,1,128]{2,0,1:T(8,128)S(1)} %bitcast.433), channel_id=1, source_target_pairs={{0,6},{1,7},{2,8},{3,9},{4,10},{5,11},{6,12},{7,13},{8,14},{9,15},... | collective-permute-start | bytes 196616 | tf_op jit(solution)/shard_map/ppermute | solution.py:32
  16.8 12.3 %collective-permute-start.6 = (f32[128,1,128]{2,0,1:T(8,128)S(1)}, f32[128,1,128]{2,0,1:T(8,128)S(1)}, u32[]{:S(2)}, u32[]{:S(2)}) collective-permute-start(f32[128,1,128]{2,0,1:T(8,128)S(1)} %bitcast.432), channel_id=1, source_target_pairs={{0,7},{1,8},{2,9},{3,10},{4,11},{5,12},{6,13},{7,14},{8,15},{9,0},... | collective-permute-start | bytes 196616 | tf_op jit(solution)/shard_map/ppermute | solution.py:32
  21.2 9.8 %collective-permute-start.7 = (f32[128,1,128]{2,0,1:T(8,128)S(1)}, f32[128,1,128]{2,0,1:T(8,128)S(1)}, u32[]{:S(2)}, u32[]{:S(2)}) collective-permute-start(f32[128,1,128]{2,0,1:T(8,128)S(1)} %bitcast.431), channel_id=1, source_target_pairs={{0,8},{1,9},{2,10},{3,11},{4,12},{5,13},{6,14},{7,15},{8,0},{9,1},... | collective-permute-start | bytes 196616 | tf_op jit(solution)/shard_map/ppermute | solution.py:32
  21.6 11.6 %collective-permute-start.8 = (f32[128,1,128]{2,0,1:T(8,128)S(1)}, f32[128,1,128]{2,0,1:T(8,128)S(1)}, u32[]{:S(2)}, u32[]{:S(2)}) collective-permute-start(f32[128,1,128]{2,0,1:T(8,128)S(1)} %bitcast.430), channel_id=1, source_target_pairs={{0,9},{1,10},{2,11},{3,12},{4,13},{5,14},{6,15},{7,0},{8,1},{9,2},... | collective-permute-start | bytes 196616 | tf_op jit(solution)/shard_map/ppermute | solution.py:32
  28.5 8.1 %collective-permute-start.9 = (f32[128,1,128]{2,0,1:T(8,128)S(1)}, f32[128,1,128]{2,0,1:T(8,128)S(1)}, u32[]{:S(2)}, u32[]{:S(2)}) collective-permute-start(f32[128,1,128]{2,0,1:T(8,128)S(1)} %bitcast.429), channel_id=1, source_target_pairs={{0,10},{1,11},{2,12},{3,13},{4,14},{5,15},{6,0},{7,1},{8,2},{9,3},... | collective-permute-start | bytes 196616 | tf_op jit(solution)/shard_map/ppermute | solution.py:32
  28.7 8.5 %collective-permute-start.10 = (f32[128,1,128]{2,0,1:T(8,128)S(1)}, f32[128,1,128]{2,0,1:T(8,128)S(1)}, u32[]{:S(2)}, u32[]{:S(2)}) collective-permute-start(f32[128,1,128]{2,0,1:T(8,128)S(1)} %bitcast.428), channel_id=1, source_target_pairs={{0,11},{1,12},{2,13},{3,14},{4,15},{5,0},{6,1},{7,2},{8,3},{9,4},{... | collective-permute-start | bytes 196616 | tf_op jit(solution)/shard_map/ppermute | solution.py:32
  29.2 8.1 %collective-permute-start.11 = (f32[128,1,128]{2,0,1:T(8,128)S(1)}, f32[128,1,128]{2,0,1:T(8,128)S(1)}, u32[]{:S(2)}, u32[]{:S(2)}) collective-permute-start(f32[128,1,128]{2,0,1:T(8,128)S(1)} %bitcast.427), channel_id=1, source_target_pairs={{0,12},{1,13},{2,14},{3,15},{4,0},{5,1},{6,2},{7,3},{8,4},{9,5},{1... | collective-permute-start | bytes 196616 | tf_op jit(solution)/shard_map/ppermute | solution.py:32
  31.0 6.2 %collective-permute-start.12 = (f32[128,1,128]{2,0,1:T(8,128)S(1)}, f32[128,1,128]{2,0,1:T(8,128)S(1)}, u32[]{:S(2)}, u32[]{:S(2)}) collective-permute-start(f32[128,1,128]{2,0,1:T(8,128)S(1)} %bitcast.426), channel_id=1, source_target_pairs={{0,13},{1,14},{2,15},{3,0},{4,1},{5,2},{6,3},{7,4},{8,5},{9,6},{10... | collective-permute-start | bytes 196616 | tf_op jit(solution)/shard_map/ppermute | solution.py:32
  33.3 6.1 %collective-permute-start.13 = (f32[128,1,128]{2,0,1:T(8,128)S(1)}, f32[128,1,128]{2,0,1:T(8,128)S(1)}, u32[]{:S(2)}, u32[]{:S(2)}) collective-permute-start(f32[128,1,128]{2,0,1:T(8,128)S(1)} %bitcast.425), channel_id=1, source_target_pairs={{0,14},{1,15},{2,0},{3,1},{4,2},{5,3},{6,4},{7,5},{8,6},{9,7},{10,... | collective-permute-start | bytes 196616 | tf_op jit(solution)/shard_map/ppermute | solution.py:32
  36.7 3.2 %collective-permute-start.14 = (f32[128,1,128]{2,0,1:T(8,128)S(1)}, f32[128,1,128]{2,0,1:T(8,128)S(1)}, u32[]{:S(2)}, u32[]{:S(2)}) collective-permute-start(f32[128,1,128]{2,0,1:T(8,128)S(1)} %bitcast.424), channel_id=1, source_target_pairs={{0,15},{1,0},{2,1},{3,2},{4,3},{5,4},{6,5},{7,6},{8,7},{9,8},{10,9... | collective-permute-start | bytes 196616 | tf_op jit(solution)/shard_map/ppermute | solution.py:32
